TPU v7x, 256 devices: a whole 4x4x8 slice. The times are simulated.
256 devices in a mesh: seq: 32 (over x_lo, z, core), tp: 8 (over y, x_hi).
Axes of the slice: x: 4 (x_hi: 2, x_lo: 2; x = x_hi * 2 + x_lo), y: 4, z: 8, core: 2. Of those that a mesh axis runs over, the one named last changes fastest.
Arguments:
- values: bfloat16 [8192, 4096], P('seq', 'tp'), may hold values from -6 to 6
- gate: bfloat16 [8192, 4096], P('seq', 'tp'), may hold values from -6 to 6
- out_grad: bfloat16 [8192, 4096], P('seq', 'tp'), may hold values from -6 to 6
- out_weight: bfloat16 [4096, 4096], P(None, 'tp'), may hold values from -0.09375 to 0.09375
- filt: float32 [8192, 4096], P('seq', 'tp'), may hold values from -6 to 6
- decay: float32 [4096], P('tp'), may hold values from 0.5 to 16
Outputs:
- d_values: bfloat16 [8192, 4096], P('seq', 'tp')
- d_gate: bfloat16 [8192, 4096], P('seq', 'tp')
- d_filt: float32 [8192, 4096], P('seq', 'tp')
- decay_grad: float32 [4096], P('tp')
- d_out_weight: float32 [4096, 4096], P('seq', 'tp')
All inputs are finite; a program needn't handle non-finite values.
Results may differ from a plain program's by a relative error of at most 0.0085.
Values may be sent and summed in bfloat16 or wider, within the bound.
A program may use at most 128 MiB of HBM per device.

v0:
```python
import math

import jax
import jax.numpy as jnp
from jax import lax
from jax.sharding import PartitionSpec as P

HIGHEST = lax.Precision.HIGHEST
TWO_PI = 2.0 * math.pi


def angles(left, right, modulus):
    index = left[:, None] * right[None, :] % modulus
    phase = index.astype(jnp.float32) * (TWO_PI / modulus)
    return jnp.cos(phase), jnp.sin(phase)


def to_channels(block, parts):
    lead = block.shape[:-2]
    tok_rows, width = block.shape[-2:]
    nd = len(lead)
    split = block.reshape(lead + (tok_rows, parts, width // parts))
    split = jnp.transpose(split, tuple(range(nd)) + (nd + 1, nd + 2, nd))
    return lax.all_to_all(split, "seq", split_axis=nd, concat_axis=nd, tiled=True)


def to_tokens(block, parts):
    lead = block.shape[:-3]
    _, sub, tok_rows = block.shape[-3:]
    nd = len(lead)
    moved = lax.all_to_all(block, "seq", split_axis=nd, concat_axis=nd, tiled=True)
    moved = moved.reshape(lead + (parts * sub, tok_rows))
    return jnp.transpose(moved, tuple(range(nd)) + (nd + 1, nd))


class Dft:
    def __init__(self, parts, rows):
        outer = 2 * parts
        self.n = outer * rows
        self.rows = rows
        p_idx = jnp.arange(parts, dtype=jnp.int32)
        k1_idx = jnp.arange(outer, dtype=jnp.int32)
        r_idx = jnp.arange(rows, dtype=jnp.int32)
        c1, s1 = angles(k1_idx, p_idx, outer)
        self.fwd_outer = jnp.concatenate([c1, -s1], axis=0)
        self.inv_outer = jnp.concatenate([c1.T, -s1.T], axis=1) / self.n
        self.twid_c, self.twid_s = angles(k1_idx, r_idx, self.n)
        gc, gs = angles(r_idx, r_idx, rows)
        self.fwd_inner = jnp.concatenate(
            [jnp.concatenate([gc, -gs], axis=1), jnp.concatenate([gs, gc], axis=1)], axis=0
        )
        self.inv_inner = jnp.concatenate(
            [jnp.concatenate([gc, gs], axis=1), jnp.concatenate([-gs, gc], axis=1)], axis=0
        )

    def forward(self, x):
        y = jnp.einsum("kp,fpcr->fkcr", self.fwd_outer, x, precision=HIGHEST)
        outer = self.fwd_outer.shape[0] // 2
        yr, yi = y[:, :outer], y[:, outer:]
        tc = self.twid_c[None, :, None, :]
        ts = self.twid_s[None, :, None, :]
        zr = yr * tc + yi * ts
        zi = yi * tc - yr * ts
        z = jnp.concatenate([zr, zi], axis=-1)
        out = jnp.einsum("fkcr,rq->fkcq", z, self.fwd_inner, precision=HIGHEST)
        return out[..., : self.rows], out[..., self.rows :]

    def inverse_real(self, zr, zi):
        z = jnp.concatenate([zr, zi], axis=-1)
        u = jnp.einsum("fkcq,qr->fkcr", z, self.inv_inner, precision=HIGHEST)
        ur, ui = u[..., : self.rows], u[..., self.rows :]
        tc = self.twid_c[None, :, None, :]
        ts = self.twid_s[None, :, None, :]
        vr = ur * tc - ui * ts
        vi = ur * ts + ui * tc
        v = jnp.concatenate([vr, vi], axis=1)
        return jnp.einsum("pk,fkcr->fpcr", self.inv_outer, v, precision=HIGHEST)


def pair_products(full_grad, gated_home, core):
    half = gated_home.shape[1] // 2
    keep_cols = lax.dynamic_slice_in_dim(gated_home, core * half, half, axis=1)
    send_cols = lax.dynamic_slice_in_dim(gated_home, (1 - core) * half, half, axis=1)
    dims = (((0,), (0,)), ((), ()))
    keep = lax.dot_general(full_grad, keep_cols, dims, preferred_element_type=jnp.float32)
    send = lax.dot_general(full_grad, send_cols, dims, preferred_element_type=jnp.float32)
    return keep, send


def pair_reduce(keep, send, core, parts, norm_scale):
    pairs = [(i, i ^ 1) for i in range(parts)]
    groups = [list(range(0, parts, 2)), list(range(1, parts, 2))]
    pair_sum = (keep + lax.ppermute(send, "seq", pairs)) * norm_scale
    rows = lax.psum_scatter(pair_sum, "seq", scatter_dimension=0, tiled=True, axis_index_groups=groups)
    block = rows.shape[0] // 2
    own = lax.dynamic_slice_in_dim(rows, core * block, block, axis=0)
    given = lax.dynamic_slice_in_dim(rows, (1 - core) * block, block, axis=0)
    got = lax.ppermute(given, "seq", pairs)
    return jnp.where(core == 0, jnp.concatenate([own, got], axis=1), jnp.concatenate([got, own], axis=1))

def on_device(values, gate, out_grad, out_weight, filt, decay):
    tok_rows, width = values.shape
    parts = lax.axis_size("seq")
    my_index = lax.axis_index("seq")
    sub = width // parts
    length = tok_rows * parts
    norm_scale = 1.0 / math.sqrt(length)

    early = to_channels(jnp.stack([values.astype(jnp.float32), filt]), parts)
    filt_c = early[1]
    gate_c = to_channels(gate, parts).astype(jnp.float32)

    full_grad = lax.all_gather(out_grad, "tp", axis=1, tiled=True)
    grad_y = jnp.dot(full_grad, out_weight, preferred_element_type=jnp.float32).astype(jnp.bfloat16)

    values_c = early[0]

    my_decay = lax.dynamic_slice_in_dim(decay, my_index * sub, sub)
    tok = (
        jnp.arange(parts, dtype=jnp.int32)[:, None, None] * tok_rows
        + jnp.arange(tok_rows, dtype=jnp.int32)[None, None, :]
    )
    position = tok.astype(jnp.float32) / length
    window = jnp.exp(-my_decay[None, :, None] * position)
    kernel = filt_c * window * norm_scale

    dft = Dft(parts, tok_rows)
    vk_r, vk_i = dft.forward(jnp.stack([values_c, kernel]))
    v_r, k_r = vk_r[0], vk_r[1]
    v_i, k_i = vk_i[0], vk_i[1]
    conv_out = dft.inverse_real((v_r * k_r - v_i * k_i)[None], (v_r * k_i + v_i * k_r)[None])[0]
    gated_out = (gate_c * conv_out).astype(jnp.bfloat16)
    gated_home = to_tokens(gated_out, parts)
    core = my_index % 2
    keep, send, grad_y = lax.optimization_barrier(pair_products(full_grad, gated_home, core) + (grad_y,))
    d_out_weight = pair_reduce(keep, send, core, parts, norm_scale)

    grad_c = to_channels(grad_y, parts).astype(jnp.float32)
    gated_grad = grad_c * gate_c
    g_r, g_i = dft.forward(gated_grad[None])
    g_r, g_i = g_r[0], g_i[0]
    prod_r = jnp.stack([k_r * g_r + k_i * g_i, v_r * g_r + v_i * g_i])
    prod_i = jnp.stack([k_r * g_i - k_i * g_r, v_r * g_i - v_i * g_r])
    conv = dft.inverse_real(prod_r, prod_i)
    conv_grad, kernel_grad = conv[0], conv[1]

    d_values = conv_grad.astype(jnp.bfloat16)
    d_gate = (grad_c * conv_out).astype(jnp.bfloat16)
    d_filt_c = kernel_grad * window * norm_scale
    decay_part = jnp.sum(position * kernel_grad * kernel, axis=(0, 2))

    back = to_tokens(
        jnp.stack([d_values.astype(jnp.float32), d_gate.astype(jnp.float32), d_filt_c]), parts
    )
    d_filt = back[2]
    spread = jnp.broadcast_to(decay_part[None, :], (parts, sub))
    gathered = lax.all_to_all(spread, "seq", split_axis=0, concat_axis=0, tiled=True)
    decay_grad = -norm_scale * gathered.reshape(width)
    return (
        back[0].astype(jnp.bfloat16), back[1].astype(jnp.bfloat16), d_filt, decay_grad, d_out_weight
    )


def solution(mesh):
    in_specs = (
        P("seq", "tp"),
        P("seq", "tp"),
        P("seq", "tp"),
        P(None, "tp"),
        P("seq", "tp"),
        P("tp"),
    )
    out_specs = (P("seq", "tp"), P("seq", "tp"), P("seq", "tp"), P("tp"), P("seq", "tp"))
    return jax.shard_map(
        on_device, mesh=mesh, in_specs=in_specs, out_specs=out_specs, check_vma=False
    )
```

profile of v0, /device:TPU:1, one launch (start us, length us, event | category | flops | bytes accessed | tf_op | source)
XLA Modules:
  0.0 233.1 jit_solution(1912060291201072105)
XLA Ops:
  7.2 1.1 copy.36
  8.3 1.2 copy.37
  9.6 1.1 copy.38
  10.7 11.0 %all-to-all-start = ((f32[2,32,16,256]{3,2,0,1:T(8,128)}), f32[2,32,16,256]{3,2,0,1:T(8,128)S(1)}, u32[]{:S(2)}, u32[]{:S(2)}) async-start(f32[2,32,16,256]{3,2,0,1:T(8,128)} %copy.38), calls=%async_computation | async-start | bytes 2097152 | tf_op jit(solution)/shard_map/all_to_all | solution.py:24
  21.8 0.7 all-gather.2.cloned.1.call-update
  22.6 0.8 copy.42
  23.4 0.8 dynamic-slice_negate_fusion
  24.3 0.7 sine_negate_fusion
  25.2 1.0 fusion.58
  26.2 1.0 fusion.56
  27.3 20.9 %all-to-all-done = f32[2,32,16,256]{3,2,0,1:T(8,128)S(1)} async-done(((f32[2,32,16,256]{3,2,0,1:T(8,128)}), f32[2,32,16,256]{3,2,0,1:T(8,128)S(1)}, u32[]{:S(2)}, u32[]{:S(2)}) %all-to-all-start) | async-done | bytes 1048608 | tf_op jit(solution)/shard_map/all_to_all | solution.py:24
  48.3 6.5 %all-to-all-start.1 = ((bf16[32,16,256]{2,1,0:T(8,128)(2,1)}), bf16[32,16,256]{2,1,0:T(8,128)(2,1)}, u32[]{:S(2)}, u32[]{:S(2)}) async-start(bf16[32,16,256]{2,1,0:T(8,128)(2,1)} %bitcast.9), calls=%async_computation.1 | async-start | bytes 524288 | tf_op jit(solution)/shard_map/all_to_all | solution.py:24
  55.6 3.6 %convolution_bitcast_fusion.2 = f32[2,128,16,256]{3,1,2,0:T(8,128)S(1)} fusion(f32[1,32,16,256]{3,1,2,0:T(8,128)S(1)} %multiply_multiply_fusion.1, f32[1,32,16,256]{3,1,2,0:T(8,128)S(1)} %copy.63, f32[64,32]{0,1:T(8,128)S(1)} %get-tuple-element.48, f32[64,32]{0,1:T(8,128)S(1)} %get-tuple-element.49), kind=kOutput, calls=%fused_computation.13 | convolution fusion | flops 402919424 | bytes 5259264 | tf_op jit(solution)/shard_map/kp,fpcr->fkcr/dot_general | solution.py:57
  59.1 0.6 multiply_add_fusion.1
  60.2 9.7 %fusion.6 = f32[2,64,16,512]{3,2,1,0:T(8,128)S(1)} fusion(f32[2,64,16,512]{3,1,2,0:T(8,128)S(1)} %pad_maximum_fusion, f32[256,256]{1,0:T(8,128)S(1)} %get-tuple-element.53, f32[256,256]{1,0:T(8,128)S(1)} %get-tuple-element.52, f32[256,256]{1,0:T(8,128)S(1)} %fusion.58), kind=kOutput, calls=%fused_computation.10 | convolution fusion | flops 6443237376 | bytes 9175040 | tf_op jit(solution)/shard_map/fkcr,rq->fkcq/dot_general | solution.py:65
  70.3 1.6 copy-done
  71.9 3.5 %fusion.17 = f32[1,64,16,512]{3,2,1,0:T(8,128)S(1)} fusion(f32[1,64,16,256]{3,2,1,0:T(8,128)S(1)} %get-tuple-element.35, f32[1,64,16,256]{3,2,1,0:T(8,128)S(1)} %get-tuple-element.34, f32[256,256]{1,0:T(8,128)S(1)} %get-tuple-element.53, f32[256,256]{1,0:T(8,128)S(1)} %fusion.58, f32[256,256]{1,0:T(8,128)S(1)} %get-tuple-element.52), kind=kOutput, calls=%fused_computation.31 | convolution fusion | flops 3222536192 | bytes 4980736 | tf_op jit(solution)/shard_map/fkcq,qr->fkcr/dot_general | solution.py:70
  76.0 4.2 %fusion.37 = (bf16[32,16,256]{2,0,1:T(8,128)(2,1)S(1)}, f32[32,16,256]{2,0,1:T(8,128)}) fusion(bf16[32,16,256]{2,1,0:T(8,128)(2,1)} %all-to-all-done.1, f32[32,64]{1,0:T(8,128)} %get-tuple-element.54, f32[32,64]{1,0:T(8,128)} %get-tuple-element.55, f32[128,16,256]{2,1,0:T(8,128)S(1)} %maximum_bitcast_fusion.2), kind=kOutput, calls=%fused_computation.63 | convolution fusion | flops 201728000 | bytes 3162112 | tf_op jit(solution)/shard_map/pk,fkcr->fpcr/dot_general | solution.py:77
  80.2 0.9 copy.45
  81.1 8.4 %all-to-all-start.2 = ((bf16[32,16,256]{2,1,0:T(8,128)(2,1)}), bf16[32,16,256]{2,1,0:T(8,128)(2,1)S(1)}, u32[]{:S(2)}, u32[]{:S(2)}) async-start(bf16[32,16,256]{2,1,0:T(8,128)(2,1)} %copy.45), calls=%async_computation.2 | async-start | bytes 524288 | tf_op jit(solution)/shard_map/all_to_all | solution.py:31
  89.6 11.8 %all-to-all-done.2 = bf16[32,16,256]{2,1,0:T(8,128)(2,1)S(1)} async-done(((bf16[32,16,256]{2,1,0:T(8,128)(2,1)}), bf16[32,16,256]{2,1,0:T(8,128)(2,1)S(1)}, u32[]{:S(2)}, u32[]{:S(2)}) %all-to-all-start.2) | async-done | bytes 262176 | tf_op jit(solution)/shard_map/all_to_all | solution.py:31
  101.4 2.5 %convolution_bitcast_fusion = f32[4096,256]{0,1:T(8,128)S(1)} fusion(bf16[256,4096]{1,0:T(8,128)(2,1)} %all-gather.2.cloned.1.call-done, bf16[512,256]{1,0:T(8,128)(2,1)S(1)} %bitcast.115, s32[]{:T(128)S(6)} %select_n.111), kind=kOutput, calls=%fused_computation | convolution fusion | flops 536870912 | bytes 6422532 | tf_op jit(solution)/shard_map/dot_general | solution.py:86
  103.9 0.7 convolution_bitcast_fusion.1
  104.6 1.5 copy-done.13
  106.1 1.2 convolution_convert_fusion
  107.3 1.6 collective-permute-start
  108.9 6.8 %collective-permute-done = f32[4096,256]{0,1:T(8,128)S(1)} collective-permute-done((f32[4096,256]{0,1:T(8,128)S(1)}, f32[4096,256]{0,1:T(8,128)S(1)}, u32[]{:S(2)}, u32[]{:S(2)}) %collective-permute-start) | collective-permute-done | bytes 4194336 | tf_op jit(solution)/shard_map/ppermute | solution.py:93
  115.7 2.6 %add_multiply_fusion = f32[4096,256]{0,1:T(8,128)} fusion(f32[4096,256]{0,1:T(8,128)S(1)} %convolution_bitcast_fusion.1, f32[4096,256]{0,1:T(8,128)S(1)} %collective-permute-done), kind=kLoop, calls=%fused_computation.12 | loop fusion | flops 2097152 | bytes 12582912 | tf_op jit(solution)/shard_map/mul | solution.py:93
  118.4 15.2 %all_to_all.31 = bf16[32,16,256]{2,1,0:T(8,128)(2,1)S(1)} all-to-all(bf16[32,16,256]{2,1,0:T(8,128)(2,1)S(1)} %bitcast.118), channel_id=1, replica_groups=mesh['seq'=32,'tp'=8] {'seq'}, dimensions={0} | all-to-all | bytes 524288 | tf_op jit(solution)/shard_map/all_to_all | solution.py:24
  133.7 2.9 %fusion.38 = f32[16,256,128]{1,2,0:T(8,128)S(1)} fusion(bf16[32,16,256]{2,1,0:T(8,128)(2,1)S(1)} %all_to_all.31, bf16[32,16,256]{2,1,0:T(8,128)(2,1)} %all-to-all-done.1, f32[64,32]{0,1:T(8,128)S(1)} %get-tuple-element.48, f32[64,32]{0,1:T(8,128)S(1)} %copy-done.8), kind=kOutput, calls=%fused_computation.64 | convolution fusion | flops 201723904 | bytes 2637824 | tf_op jit(solution)/shard_map/kp,fpcr->fkcr/dot_general | solution.py:57
  136.5 1.2 copy.88
  138.2 3.5 %fusion.16 = f32[1,64,16,512]{3,2,1,0:T(8,128)S(1)} fusion(f32[1,64,16,256]{3,2,1,0:T(8,128)S(1)} %get-tuple-element.37, f32[1,64,16,256]{3,2,1,0:T(8,128)S(1)} %get-tuple-element.36, f32[256,256]{1,0:T(8,128)S(1)} %get-tuple-element.53, f32[256,256]{1,0:T(8,128)S(1)} %get-tuple-element.52, f32[256,256]{1,0:T(8,128)S(1)} %fusion.58), kind=kOutput, calls=%fused_computation.30 | convolution fusion | flops 3222536192 | bytes 4980736 | tf_op jit(solution)/shard_map/fkcr,rq->fkcq/dot_general | solution.py:65
  141.7 0.7 multiply_add_fusion.3
  143.0 9.1 %fusion.4 = f32[2,64,16,512]{3,1,2,0:T(8,128)S(1)} fusion(f32[2,64,16,512]{3,2,1,0:T(8,128)S(1)} %maximum_maximum_fusion, f32[256,256]{1,0:T(8,128)S(1)} %get-tuple-element.53, f32[256,256]{1,0:T(8,128)S(1)} %fusion.58, f32[256,256]{1,0:T(8,128)S(1)} %get-tuple-element.52), kind=kOutput, calls=%fused_computation.8 | convolution fusion | flops 6443237376 | bytes 9175040 | tf_op jit(solution)/shard_map/fkcq,qr->fkcr/dot_general | solution.py:70
  152.2 0.7 multiply_subtract_fusion
  152.9 2.4 %fusion.18 = f32[2,32,16,256]{3,1,2,0:T(8,128)S(1)} fusion(f32[2,64,16,256]{3,1,2,0:T(8,128)S(1)} %get-tuple-element.31, f32[2,64,16,256]{3,1,2,0:T(8,128)S(1)} %get-tuple-element.30, f32[32,64]{1,0:T(8,128)S(1)} %copy-done.9, f32[32,64]{1,0:T(8,128)S(1)} %copy-done.10), kind=kOutput, calls=%fused_computation.37 | convolution fusion | flops 403709952 | bytes 5259264 | tf_op jit(solution)/shard_map/pk,fkcr->fpcr/dot_general | solution.py:77
  155.9 0.6 broadcast_in_dim.2
  156.5 5.3 %all-to-all-start.5 = ((f32[32,1,16]{2,1,0:T(1,128)}), f32[32,1,16]{2,1,0:T(1,128)S(1)}, u32[]{:S(2)}, u32[]{:S(2)}) async-start(f32[32,1,16]{2,1,0:T(1,128)} %broadcast_in_dim.2), calls=%async_computation.5 | async-start | bytes 32768 | tf_op jit(solution)/shard_map/all_to_all | solution.py:157
  162.3 2.1 copy.51
  164.4 5.3 %all-to-all-done.5 = f32[32,1,16]{2,1,0:T(1,128)S(1)} async-done(((f32[32,1,16]{2,1,0:T(1,128)}), f32[32,1,16]{2,1,0:T(1,128)S(1)}, u32[]{:S(2)}, u32[]{:S(2)}) %all-to-all-start.5) | async-done | bytes 2080 | tf_op jit(solution)/shard_map/all_to_all | solution.py:157
  169.6 4.4 %all-to-all-start.4 = ((f32[3,32,16,256]{3,2,0,1:T(8,128)}), f32[3,32,16,256]{3,2,0,1:T(8,128)S(1)}, u32[]{:S(2)}, u32[]{:S(2)}) async-start(f32[3,32,16,256]{3,2,0,1:T(8,128)} %copy.51), calls=%async_computation.4 | async-start | bytes 3145728 | tf_op jit(solution)/shard_map/all_to_all | solution.py:31
  174.1 0.7 mul.635
  174.8 45.9 %all-to-all-done.4 = f32[3,32,16,256]{3,2,0,1:T(8,128)S(1)} async-done(((f32[3,32,16,256]{3,2,0,1:T(8,128)}), f32[3,32,16,256]{3,2,0,1:T(8,128)S(1)}, u32[]{:S(2)}, u32[]{:S(2)}) %all-to-all-start.4) | async-done | bytes 1572896 | tf_op jit(solution)/shard_map/all_to_all | solution.py:31
  221.0 0.8 copy.53
  221.9 0.8 copy.54
  222.7 1.0 constant_dynamic-slice_fusion.1
  224.0 1.0 copy.55
  225.2 0.8 copy.56
  (61 shorter events, 5.8 us)
Async XLA Ops:
  9.6 12.9 %copy-start.6 = (bf16[256,512]{1,0:T(8,128)(2,1)S(1)}, bf16[256,512]{1,0:T(8,128)(2,1)}, u32[]{:S(2)}) copy-start(bf16[256,512]{1,0:T(8,128)(2,1)} %param.7) | copy-start | bytes 786436
  10.7 37.5 %all-to-all-start = ((f32[2,32,16,256]{3,2,0,1:T(8,128)}), f32[2,32,16,256]{3,2,0,1:T(8,128)S(1)}, u32[]{:S(2)}, u32[]{:S(2)}) async-start(f32[2,32,16,256]{3,2,0,1:T(8,128)} %copy.38), calls=%async_computation | async-start | bytes 2097152 | tf_op jit(solution)/shard_map/all_to_all | solution.py:24
  21.8 79.6 %all-gather.2.cloned.1.call-start = ((), (), s32[]{:S(2)}) async-start(), calls=%async_computation.7 | async-start | bytes 2359296 | tf_op jit(solution)/shard_map/all_gather | solution.py:113
  24.2 31.0 %copy-start.11 = (f32[16]{0:T(128)}, f32[16]{0:T(128)S(1)}, u32[]{:S(2)}) copy-start(f32[16]{0:T(128)S(1)} %dynamic-slice_negate_fusion) | copy-start | bytes 196
  24.2 31.3 %copy-start.7 = (f32[64,32]{0,1:T(8,128)}, f32[64,32]{0,1:T(8,128)S(1)}, u32[]{:S(2)}) copy-start(f32[64,32]{0,1:T(8,128)S(1)} %get-tuple-element.49) | copy-start | bytes 24580
  27.3 28.2 %copy-start.4 = (f32[32,256]{1,0:T(8,128)}, f32[32,256]{1,0:T(8,128)S(1)}, u32[]{:S(2)}) copy-start(f32[32,256]{1,0:T(8,128)S(1)} %convert_multiply_fusion.4) | copy-start | bytes 98308
  48.3 27.7 %all-to-all-start.1 = ((bf16[32,16,256]{2,1,0:T(8,128)(2,1)}), bf16[32,16,256]{2,1,0:T(8,128)(2,1)}, u32[]{:S(2)}, u32[]{:S(2)}) async-start(bf16[32,16,256]{2,1,0:T(8,128)(2,1)} %bitcast.9), calls=%async_computation.1 | async-start | bytes 524288 | tf_op jit(solution)/shard_map/all_to_all | solution.py:24
  69.9 2.0 copy-start
  81.1 20.3 %all-to-all-start.2 = ((bf16[32,16,256]{2,1,0:T(8,128)(2,1)}), bf16[32,16,256]{2,1,0:T(8,128)(2,1)S(1)}, u32[]{:S(2)}, u32[]{:S(2)}) async-start(bf16[32,16,256]{2,1,0:T(8,128)(2,1)} %copy.45), calls=%async_computation.2 | async-start | bytes 524288 | tf_op jit(solution)/shard_map/all_to_all | solution.py:31
  89.5 133.2 %reduce-scatter.2.cloned.1.call-start = ((), (), s32[]{:S(2)}) async-start(), calls=%async_computation.8 | async-start | bytes 4456448 | tf_op jit(solution)/shard_map/reduce_scatter | solution.py:94
  101.4 2.5 %copy-start.2 = (bf16[256,4096]{1,0:T(8,128)(2,1)S(1)}, bf16[256,4096]{1,0:T(8,128)(2,1)}, u32[]{:S(2)}) copy-start(bf16[256,4096]{1,0:T(8,128)(2,1)} %all-gather.2.cloned.1.call-done) | copy-start | bytes 6291460
  103.9 2.2 copy-start.13
  107.3 8.4 %collective-permute-start = (f32[4096,256]{0,1:T(8,128)S(1)}, f32[4096,256]{0,1:T(8,128)S(1)}, u32[]{:S(2)}, u32[]{:S(2)}) collective-permute-start(f32[4096,256]{0,1:T(8,128)S(1)} %convolution_bitcast_fusion), channel_id=1, source_target_pairs={{0,8},{8,0},{16,24},{24,16},{32,40},{40,32},{48,56},{56,48},{64,72... | collective-permute-start | bytes 12582920 | tf_op jit(solution)/shard_map/ppermute | solution.py:93
  118.3 15.4 %copy-start.8 = (f32[64,32]{0,1:T(8,128)S(1)}, f32[64,32]{0,1:T(8,128)}, u32[]{:S(2)}) copy-start(f32[64,32]{0,1:T(8,128)} %copy-done.7) | copy-start | bytes 24580
  138.2 3.5 %copy-start.1 = (f32[2,64,16,512]{3,2,1,0:T(8,128)S(1)}, f32[2,64,16,512]{3,2,1,0:T(8,128)}, u32[]{:S(2)}) copy-start(f32[2,64,16,512]{3,2,1,0:T(8,128)} %copy-done) | copy-start | bytes 12582916
  152.1 0.7 copy-start.9
  152.2 0.7 copy-start.10
  152.9 2.4 %copy-start.5 = (f32[32,256]{1,0:T(8,128)S(1)}, f32[32,256]{1,0:T(8,128)}, u32[]{:S(2)}) copy-start(f32[32,256]{1,0:T(8,128)} %copy-done.4) | copy-start | bytes 98308
  152.9 2.4 %copy-start.12 = (f32[16]{0:T(128)S(1)}, f32[16]{0:T(128)}, u32[]{:S(2)}) copy-start(f32[16]{0:T(128)} %copy-done.11) | copy-start | bytes 196
  155.3 6.7 %copy-start.3 = (f32[32,16,256]{2,0,1:T(8,128)S(1)}, f32[32,16,256]{2,0,1:T(8,128)}, u32[]{:S(2)}) copy-start(f32[32,16,256]{2,0,1:T(8,128)} %get-tuple-element.47) | copy-start | bytes 1572868
  156.5 13.2 %all-to-all-start.5 = ((f32[32,1,16]{2,1,0:T(1,128)}), f32[32,1,16]{2,1,0:T(1,128)S(1)}, u32[]{:S(2)}, u32[]{:S(2)}) async-start(f32[32,1,16]{2,1,0:T(1,128)} %broadcast_in_dim.2), calls=%async_computation.5 | async-start | bytes 32768 | tf_op jit(solution)/shard_map/all_to_all | solution.py:157
  169.6 51.1 %all-to-all-start.4 = ((f32[3,32,16,256]{3,2,0,1:T(8,128)}), f32[3,32,16,256]{3,2,0,1:T(8,128)S(1)}, u32[]{:S(2)}, u32[]{:S(2)}) async-start(f32[3,32,16,256]{3,2,0,1:T(8,128)} %copy.51), calls=%async_computation.4 | async-start | bytes 3145728 | tf_op jit(solution)/shard_map/all_to_all | solution.py:31
  223.7 1.4 collective-permute-start.1
Sparse Core Ops, SparseCore 0:
  25.1 62.3 all-gather.1
  118.4 81.0 reduce-scatter.1
where the time goes:
time: 237 us; the launch traced here: 233 us
  waiting for transfers between devices  91.6 us (39%)
  matrix products  43.2 us (18%)
  starting transfers between devices  37.6 us (16%)
  local copies, waits for them, and re-layouts  18.1 us (8%)
  blocking collectives  15.2 us (6%)
  between operations  14.8 us (6%)
  other arithmetic  12.5 us (5%)
    all_to_all x2, waiting for transfers between devices, to_tokens(): lax.all_to_all(block, 'seq', split_axis=nd, concat_axis=nd, tiled=True)  57.8 us
    all_to_all x2, waiting for transfers between devices, to_channels(): lax.all_to_all(split, 'seq', split_axis=nd, concat_axis=nd, tiled=True)  20.9 us
    all_to_all x2, starting transfers between devices, to_channels(): lax.all_to_all(split, 'seq', split_axis=nd, concat_axis=nd, tiled=True)  17.5 us
    all_to_all x1, blocking collectives, to_channels(): lax.all_to_all(split, 'seq', split_axis=nd, concat_axis=nd, tiled=True)  15.2 us
    dot_general x2, matrix products, forward(): out = jnp.einsum('fkcr,rq->fkcq', z, self.fwd_inner, precision=HIGHEST)  13.1 us
    all_to_all x2, starting transfers between devices, to_tokens(): lax.all_to_all(block, 'seq', split_axis=nd, concat_axis=nd, tiled=True)  12.8 us
    dot_general x2, matrix products, inverse_real(): u = jnp.einsum('fkcq,qr->fkcr', z, self.inv_inner, precision=HIGHEST)  12.6 us
    unnamed x36, local copies, waits for them, and re-layouts  10.2 us
  transfers between devices with their start and end apart: 9, of which 6 were waited for; matrix products, arithmetic and copies ran while one was open for 25% of the time, Pallas kernels for 0%

commit v1 on v0

--- a/solution.py
+++ b/solution.py
@@ -5,7 +5,7 @@
 from jax import lax
 from jax.sharding import PartitionSpec as P
 
-HIGHEST = lax.Precision.HIGHEST
+DFT_PRECISION = lax.Precision.HIGH
 TWO_PI = 2.0 * math.pi
 
 
@@ -54,7 +54,7 @@
         )
 
     def forward(self, x):
-        y = jnp.einsum("kp,fpcr->fkcr", self.fwd_outer, x, precision=HIGHEST)
+        y = jnp.einsum("kp,fpcr->fkcr", self.fwd_outer, x, precision=DFT_PRECISION)
         outer = self.fwd_outer.shape[0] // 2
         yr, yi = y[:, :outer], y[:, outer:]
         tc = self.twid_c[None, :, None, :]
@@ -62,19 +62,19 @@
         zr = yr * tc + yi * ts
         zi = yi * tc - yr * ts
         z = jnp.concatenate([zr, zi], axis=-1)
-        out = jnp.einsum("fkcr,rq->fkcq", z, self.fwd_inner, precision=HIGHEST)
+        out = jnp.einsum("fkcr,rq->fkcq", z, self.fwd_inner, precision=DFT_PRECISION)
         return out[..., : self.rows], out[..., self.rows :]
 
     def inverse_real(self, zr, zi):
         z = jnp.concatenate([zr, zi], axis=-1)
-        u = jnp.einsum("fkcq,qr->fkcr", z, self.inv_inner, precision=HIGHEST)
+        u = jnp.einsum("fkcq,qr->fkcr", z, self.inv_inner, precision=DFT_PRECISION)
         ur, ui = u[..., : self.rows], u[..., self.rows :]
         tc = self.twid_c[None, :, None, :]
         ts = self.twid_s[None, :, None, :]
         vr = ur * tc - ui * ts
         vi = ur * ts + ui * tc
         v = jnp.concatenate([vr, vi], axis=1)
-        return jnp.einsum("pk,fkcr->fpcr", self.inv_outer, v, precision=HIGHEST)
+        return jnp.einsum("pk,fkcr->fpcr", self.inv_outer, v, precision=DFT_PRECISION)
 
 
 def pair_products(full_grad, gated_home, core):

time: 237 us -> 239 us (level)
  matrix products: 43.2 us -> 38.9 us
  waiting for transfers between devices: 91.6 us -> 94.9 us
    dot_general x8, matrix products: 38.8 us -> 34.5 us  [the longest x2 16.5 us: inverse_real(): jnp.einsum('pk,fkcr->fpcr', self.inv_outer, v, precision=DFT_PRECISION)]
    all_to_all x2, waiting for transfers between devices: 57.8 us -> 61.2 us  [to_tokens(): lax.all_to_all(block, 'seq', split_axis=nd, concat_axis=nd, tiled=True)]
  transfers between devices with their start and end apart: 9 -> 9, of which waited for: 6 -> 5; matrix products, arithmetic and copies ran while one was open for 25% -> 23% of each run, Pallas kernels for 0% -> 0%
where the time goes in v1:
time: 239 us; the launch traced here: 234 us
  waiting for transfers between devices  94.9 us (40%)
  starting transfers between devices  39.3 us (16%)
  matrix products  38.9 us (16%)
  local copies, waits for them, and re-layouts  18.5 us (8%)
  blocking collectives  15.2 us (6%)
  between operations  14.8 us (6%)
  other arithmetic  12.7 us (5%)
    all_to_all x2, waiting for transfers between devices, to_tokens(): lax.all_to_all(block, 'seq', split_axis=nd, concat_axis=nd, tiled=True)  61.2 us
    all_to_all x2, waiting for transfers between devices, to_channels(): lax.all_to_all(split, 'seq', split_axis=nd, concat_axis=nd, tiled=True)  20.9 us
    all_to_all x2, starting transfers between devices, to_channels(): lax.all_to_all(split, 'seq', split_axis=nd, concat_axis=nd, tiled=True)  17.7 us
    dot_general x2, matrix products, inverse_real(): jnp.einsum('pk,fkcr->fpcr', self.inv_outer, v, precision=DFT_PRECISION)  16.5 us
    all_to_all x1, blocking collectives, to_channels(): lax.all_to_all(split, 'seq', split_axis=nd, concat_axis=nd, tiled=True)  15.2 us
    all_to_all x2, starting transfers between devices, to_tokens(): lax.all_to_all(block, 'seq', split_axis=nd, concat_axis=nd, tiled=True)  12.8 us
    unnamed x36, local copies, waits for them, and re-layouts  10.6 us
    dot_general x2, matrix products, forward(): jnp.einsum('fkcr,rq->fkcq', z, self.fwd_inner, precision=DFT_PRECISION)  7.02 us
  transfers between devices with their start and end apart: 9, of which 5 were waited for; matrix products, arithmetic and copies ran while one was open for 23% of the time, Pallas kernels for 0%

profile of v1, /device:TPU:1, one launch (start us, length us, event | category | flops | bytes accessed | tf_op | source)
XLA Modules:
  0.0 234.3 jit_solution(10804319203788397540)
XLA Ops:
  7.2 1.1 copy.36
  8.3 1.2 copy.37
  9.6 1.1 copy.38
  10.7 11.0 %all-to-all-start = ((f32[2,32,16,256]{3,2,0,1:T(8,128)}), f32[2,32,16,256]{3,2,0,1:T(8,128)S(1)}, u32[]{:S(2)}, u32[]{:S(2)}) async-start(f32[2,32,16,256]{3,2,0,1:T(8,128)} %copy.38), calls=%async_computation | async-start | bytes 2097152 | tf_op jit(solution)/shard_map/all_to_all | solution.py:24
  21.8 0.7 all-gather.2.cloned.1.call-update
  22.6 0.8 copy.42
  23.4 0.8 dynamic-slice_negate_fusion
  24.3 0.7 sine_negate_fusion
  25.2 1.0 fusion.58
  26.2 1.0 fusion.56
  27.3 20.9 %all-to-all-done = f32[2,32,16,256]{3,2,0,1:T(8,128)S(1)} async-done(((f32[2,32,16,256]{3,2,0,1:T(8,128)}), f32[2,32,16,256]{3,2,0,1:T(8,128)S(1)}, u32[]{:S(2)}, u32[]{:S(2)}) %all-to-all-start) | async-done | bytes 1048608 | tf_op jit(solution)/shard_map/all_to_all | solution.py:24
  48.3 6.7 %all-to-all-start.1 = ((bf16[32,16,256]{2,1,0:T(8,128)(2,1)}), bf16[32,16,256]{2,1,0:T(8,128)(2,1)}, u32[]{:S(2)}, u32[]{:S(2)}) async-start(bf16[32,16,256]{2,1,0:T(8,128)(2,1)} %bitcast.9), calls=%async_computation.1 | async-start | bytes 524288 | tf_op jit(solution)/shard_map/all_to_all | solution.py:24
  55.8 1.9 convolution_bitcast_fusion.2
  58.8 5.2 %fusion.6 = f32[2,64,16,512]{3,2,1,0:T(8,128)S(1)} fusion(f32[2,64,16,512]{3,1,2,0:T(8,128)S(1)} %pad_maximum_fusion, f32[256,256]{1,0:T(8,128)S(1)} %get-tuple-element.53, f32[256,256]{1,0:T(8,128)S(1)} %get-tuple-element.52, f32[256,256]{1,0:T(8,128)S(1)} %fusion.58), kind=kOutput, calls=%fused_computation.10 | convolution fusion | flops 3222011904 | bytes 9175040 | tf_op jit(solution)/shard_map/fkcr,rq->fkcq/dot_general | solution.py:65
  64.4 1.6 copy-done
  66.0 1.8 fusion.17
  68.4 15.3 %fusion.37 = (bf16[32,16,256]{2,0,1:T(8,128)(2,1)S(1)}, f32[32,16,256]{2,0,1:T(8,128)}) fusion(bf16[32,16,256]{2,1,0:T(8,128)(2,1)} %all-to-all-done.1, f32[32,64]{1,0:T(8,128)} %get-tuple-element.54, f32[32,64]{1,0:T(8,128)} %get-tuple-element.55, f32[128,16,256]{2,1,0:T(8,128)S(1)} %maximum_bitcast_fusion.2), kind=kOutput, calls=%fused_computation.63 | convolution fusion | flops 101064704 | bytes 3162112 | tf_op jit(solution)/shard_map/pk,fkcr->fpcr/dot_general | solution.py:77
  83.7 0.9 copy.45
  84.6 8.4 %all-to-all-start.2 = ((bf16[32,16,256]{2,1,0:T(8,128)(2,1)}), bf16[32,16,256]{2,1,0:T(8,128)(2,1)S(1)}, u32[]{:S(2)}, u32[]{:S(2)}) async-start(bf16[32,16,256]{2,1,0:T(8,128)(2,1)} %copy.45), calls=%async_computation.2 | async-start | bytes 524288 | tf_op jit(solution)/shard_map/all_to_all | solution.py:31
  93.0 11.8 %all-to-all-done.2 = bf16[32,16,256]{2,1,0:T(8,128)(2,1)S(1)} async-done(((bf16[32,16,256]{2,1,0:T(8,128)(2,1)}), bf16[32,16,256]{2,1,0:T(8,128)(2,1)S(1)}, u32[]{:S(2)}, u32[]{:S(2)}) %all-to-all-start.2) | async-done | bytes 262176 | tf_op jit(solution)/shard_map/all_to_all | solution.py:31
  104.9 2.5 %convolution_bitcast_fusion = f32[4096,256]{0,1:T(8,128)S(1)} fusion(bf16[256,4096]{1,0:T(8,128)(2,1)} %all-gather.2.cloned.1.call-done, bf16[512,256]{1,0:T(8,128)(2,1)S(1)} %bitcast.115, s32[]{:T(128)S(6)} %select_n.111), kind=kOutput, calls=%fused_computation | convolution fusion | flops 536870912 | bytes 6422532 | tf_op jit(solution)/shard_map/dot_general | solution.py:86
  107.4 0.7 convolution_bitcast_fusion.1
  108.1 1.5 copy-done.13
  109.6 1.2 convolution_convert_fusion
  110.8 1.6 collective-permute-start
  112.4 6.8 %collective-permute-done = f32[4096,256]{0,1:T(8,128)S(1)} collective-permute-done((f32[4096,256]{0,1:T(8,128)S(1)}, f32[4096,256]{0,1:T(8,128)S(1)}, u32[]{:S(2)}, u32[]{:S(2)}) %collective-permute-start) | collective-permute-done | bytes 4194336 | tf_op jit(solution)/shard_map/ppermute | solution.py:93
  119.2 2.6 %add_multiply_fusion = f32[4096,256]{0,1:T(8,128)} fusion(f32[4096,256]{0,1:T(8,128)S(1)} %convolution_bitcast_fusion.1, f32[4096,256]{0,1:T(8,128)S(1)} %collective-permute-done), kind=kLoop, calls=%fused_computation.12 | loop fusion | flops 2097152 | bytes 12582912 | tf_op jit(solution)/shard_map/mul | solution.py:93
  121.9 15.2 %all_to_all.31 = bf16[32,16,256]{2,1,0:T(8,128)(2,1)S(1)} all-to-all(bf16[32,16,256]{2,1,0:T(8,128)(2,1)S(1)} %bitcast.118), channel_id=1, replica_groups=mesh['seq'=32,'tp'=8] {'seq'}, dimensions={0} | all-to-all | bytes 524288 | tf_op jit(solution)/shard_map/all_to_all | solution.py:24
  137.1 2.0 fusion.38
  139.2 1.2 copy.88
  140.9 1.8 fusion.16
  143.1 0.7 multiply_add_fusion.3
  144.4 5.2 %fusion.4 = f32[2,64,16,512]{3,1,2,0:T(8,128)S(1)} fusion(f32[2,64,16,512]{3,2,1,0:T(8,128)S(1)} %maximum_maximum_fusion, f32[256,256]{1,0:T(8,128)S(1)} %get-tuple-element.53, f32[256,256]{1,0:T(8,128)S(1)} %fusion.58, f32[256,256]{1,0:T(8,128)S(1)} %get-tuple-element.52), kind=kOutput, calls=%fused_computation.8 | convolution fusion | flops 3222011904 | bytes 9175040 | tf_op jit(solution)/shard_map/fkcq,qr->fkcr/dot_general | solution.py:70
  149.6 0.7 multiply_subtract_fusion
  150.3 1.2 fusion.18
  151.6 0.7 fusion.42
  152.9 5.3 %all-to-all-start.5 = ((f32[32,1,16]{2,1,0:T(1,128)}), f32[32,1,16]{2,1,0:T(1,128)S(1)}, u32[]{:S(2)}, u32[]{:S(2)}) async-start(f32[32,1,16]{2,1,0:T(1,128)} %broadcast_in_dim.2), calls=%async_computation.5 | async-start | bytes 32768 | tf_op jit(solution)/shard_map/all_to_all | solution.py:157
  158.7 2.1 copy.51
  160.8 5.3 %all-to-all-done.5 = f32[32,1,16]{2,1,0:T(1,128)S(1)} async-done(((f32[32,1,16]{2,1,0:T(1,128)}), f32[32,1,16]{2,1,0:T(1,128)S(1)}, u32[]{:S(2)}, u32[]{:S(2)}) %all-to-all-start.5) | async-done | bytes 2080 | tf_op jit(solution)/shard_map/all_to_all | solution.py:157
  166.1 4.4 %all-to-all-start.4 = ((f32[3,32,16,256]{3,2,0,1:T(8,128)}), f32[3,32,16,256]{3,2,0,1:T(8,128)S(1)}, u32[]{:S(2)}, u32[]{:S(2)}) async-start(f32[3,32,16,256]{3,2,0,1:T(8,128)} %copy.51), calls=%async_computation.4 | async-start | bytes 3145728 | tf_op jit(solution)/shard_map/all_to_all | solution.py:31
  170.6 0.7 mul.635
  171.2 49.3 %all-to-all-done.4 = f32[3,32,16,256]{3,2,0,1:T(8,128)S(1)} async-done(((f32[3,32,16,256]{3,2,0,1:T(8,128)}), f32[3,32,16,256]{3,2,0,1:T(8,128)S(1)}, u32[]{:S(2)}, u32[]{:S(2)}) %all-to-all-start.4) | async-done | bytes 1572896 | tf_op jit(solution)/shard_map/all_to_all | solution.py:31
  220.9 0.8 copy.53
  221.7 0.8 copy.54
  222.5 1.0 constant_dynamic-slice_fusion.1
  223.5 1.8 collective-permute-start.1
  225.4 1.0 copy.55
  226.4 0.8 copy.56
  (61 shorter events, 6.5 us)
Async XLA Ops:
  9.6 12.9 %copy-start.6 = (bf16[256,512]{1,0:T(8,128)(2,1)S(1)}, bf16[256,512]{1,0:T(8,128)(2,1)}, u32[]{:S(2)}) copy-start(bf16[256,512]{1,0:T(8,128)(2,1)} %param.7) | copy-start | bytes 786436
  10.7 37.5 %all-to-all-start = ((f32[2,32,16,256]{3,2,0,1:T(8,128)}), f32[2,32,16,256]{3,2,0,1:T(8,128)S(1)}, u32[]{:S(2)}, u32[]{:S(2)}) async-start(f32[2,32,16,256]{3,2,0,1:T(8,128)} %copy.38), calls=%async_computation | async-start | bytes 2097152 | tf_op jit(solution)/shard_map/all_to_all | solution.py:24
  21.8 83.1 %all-gather.2.cloned.1.call-start = ((), (), s32[]{:S(2)}) async-start(), calls=%async_computation.7 | async-start | bytes 2359296 | tf_op jit(solution)/shard_map/all_gather | solution.py:113
  24.2 31.2 %copy-start.11 = (f32[16]{0:T(128)}, f32[16]{0:T(128)S(1)}, u32[]{:S(2)}) copy-start(f32[16]{0:T(128)S(1)} %dynamic-slice_negate_fusion) | copy-start | bytes 196
  24.2 31.5 %copy-start.7 = (f32[64,32]{0,1:T(8,128)}, f32[64,32]{0,1:T(8,128)S(1)}, u32[]{:S(2)}) copy-start(f32[64,32]{0,1:T(8,128)S(1)} %get-tuple-element.49) | copy-start | bytes 24580
  27.3 28.4 %copy-start.4 = (f32[32,256]{1,0:T(8,128)}, f32[32,256]{1,0:T(8,128)S(1)}, u32[]{:S(2)}) copy-start(f32[32,256]{1,0:T(8,128)S(1)} %convert_multiply_fusion.4) | copy-start | bytes 98308
  48.3 20.2 %all-to-all-start.1 = ((bf16[32,16,256]{2,1,0:T(8,128)(2,1)}), bf16[32,16,256]{2,1,0:T(8,128)(2,1)}, u32[]{:S(2)}, u32[]{:S(2)}) async-start(bf16[32,16,256]{2,1,0:T(8,128)(2,1)} %bitcast.9), calls=%async_computation.1 | async-start | bytes 524288 | tf_op jit(solution)/shard_map/all_to_all | solution.py:24
  64.0 2.0 copy-start
  84.6 20.3 %all-to-all-start.2 = ((bf16[32,16,256]{2,1,0:T(8,128)(2,1)}), bf16[32,16,256]{2,1,0:T(8,128)(2,1)S(1)}, u32[]{:S(2)}, u32[]{:S(2)}) async-start(bf16[32,16,256]{2,1,0:T(8,128)(2,1)} %copy.45), calls=%async_computation.2 | async-start | bytes 524288 | tf_op jit(solution)/shard_map/all_to_all | solution.py:31
  93.0 129.6 %reduce-scatter.2.cloned.1.call-start = ((), (), s32[]{:S(2)}) async-start(), calls=%async_computation.8 | async-start | bytes 4456448 | tf_op jit(solution)/shard_map/reduce_scatter | solution.py:94
  104.9 2.5 %copy-start.2 = (bf16[256,4096]{1,0:T(8,128)(2,1)S(1)}, bf16[256,4096]{1,0:T(8,128)(2,1)}, u32[]{:S(2)}) copy-start(bf16[256,4096]{1,0:T(8,128)(2,1)} %all-gather.2.cloned.1.call-done) | copy-start | bytes 6291460
  107.4 2.2 copy-start.13
  110.8 8.4 %collective-permute-start = (f32[4096,256]{0,1:T(8,128)S(1)}, f32[4096,256]{0,1:T(8,128)S(1)}, u32[]{:S(2)}, u32[]{:S(2)}) collective-permute-start(f32[4096,256]{0,1:T(8,128)S(1)} %convolution_bitcast_fusion), channel_id=1, source_target_pairs={{0,8},{8,0},{16,24},{24,16},{32,40},{40,32},{48,56},{56,48},{64,72... | collective-permute-start | bytes 12582920 | tf_op jit(solution)/shard_map/ppermute | solution.py:93
  121.7 15.4 %copy-start.8 = (f32[64,32]{0,1:T(8,128)S(1)}, f32[64,32]{0,1:T(8,128)}, u32[]{:S(2)}) copy-start(f32[64,32]{0,1:T(8,128)} %copy-done.7) | copy-start | bytes 24580
  140.8 2.2 copy-start.1
  149.6 0.7 copy-start.9
  149.6 0.7 copy-start.10
  150.3 1.2 copy-start.5
  150.3 1.2 copy-start.12
  151.6 6.8 %copy-start.3 = (f32[32,16,256]{2,0,1:T(8,128)S(1)}, f32[32,16,256]{2,0,1:T(8,128)}, u32[]{:S(2)}) copy-start(f32[32,16,256]{2,0,1:T(8,128)} %get-tuple-element.47) | copy-start | bytes 1572868
  152.9 13.2 %all-to-all-start.5 = ((f32[32,1,16]{2,1,0:T(1,128)}), f32[32,1,16]{2,1,0:T(1,128)S(1)}, u32[]{:S(2)}, u32[]{:S(2)}) async-start(f32[32,1,16]{2,1,0:T(1,128)} %broadcast_in_dim.2), calls=%async_computation.5 | async-start | bytes 32768 | tf_op jit(solution)/shard_map/all_to_all | solution.py:157
  166.1 54.5 %all-to-all-start.4 = ((f32[3,32,16,256]{3,2,0,1:T(8,128)}), f32[3,32,16,256]{3,2,0,1:T(8,128)S(1)}, u32[]{:S(2)}, u32[]{:S(2)}) async-start(f32[3,32,16,256]{3,2,0,1:T(8,128)} %copy.51), calls=%async_computation.4 | async-start | bytes 3145728 | tf_op jit(solution)/shard_map/all_to_all | solution.py:31
  223.5 2.8 %collective-permute-start.1 = (f32[128,256]{0,1:T(8,128)S(1)}, f32[128,256]{0,1:T(8,128)S(1)}, u32[]{:S(2)}, u32[]{:S(2)}) collective-permute-start(f32[128,256]{0,1:T(8,128)S(1)} %get-tuple-element.45), channel_id=1, source_target_pairs={{0,8},{8,0},{16,24},{24,16},{32,40},{40,32},{48,56},{56,48},{64,72... | collective-permute-start | bytes 393224 | tf_op jit(solution)/shard_map/ppermute | solution.py:98
Sparse Core Ops, SparseCore 0:
  25.1 62.3 all-gather.1
  121.9 91.7 reduce-scatter.1
